TPU v7x, 32 devices: a whole 2x2x4 slice. The times are simulated.
32 devices in a mesh: groups: 2 (over x), psg: 16 (over z, y, core).
Axes of the slice: x: 2, y: 2, z: 4, core: 2. Of those that a mesh axis runs over, the one named last changes fastest.
Arguments:
- queries: bfloat16 [64, 32, 128], P(('groups', 'psg')), parts along dimension 0, may hold values from -0.29882812 to 0.29882812
- candidates: int32 [64, 512], P(('groups', 'psg')), parts along dimension 0, may hold values from 0 to 159
- centroids: bfloat16 [8192, 128], P('psg'), may hold values from -6 to 6
- bucket_weights: float32 [4, 128], replicated, may hold values from -1 to 1
- centroid_shard: int32 [32768, 1], P('psg'), may hold values from 0 to 15; in each aligned block of 2048 rows (0 to 2047, 2048 to 4095, ...) at most 256 rows name the same one
- centroid_row: int32 [32768], P('psg'), may hold values from 0 to 511
- residual_codes: int32 [32768, 128], P('psg'), may hold values from 0 to 3
- tile_count: int32 [160], replicated, may hold values from 1 to 3, 256 in all
- last_fill: int32 [160], replicated, may hold values from 1 to 128
Outputs:
- scores: float32 [64, 512], P(('groups', 'psg')), parts along dimension 0
There are 2 independent parts, one for each index of `groups`. A program takes and returns all parts, laid end to end along the dimension named above; an argument that names none is the same for every part. Nothing has to cross between parts.
Inputs may be any that keep to these rules, and one draw needn't show every extreme that they name: `tile_count`: tiles are numbered along psg, device k holding tiles k * 16 onward; the counts sum to 256, so a passage may continue on the next device. `centroid_shard`: among the 2048 token slots of one device, at most 256 name the same device; on some device some value is named exactly 256 times.
All inputs are finite; a program needn't handle non-finite values.
Results may differ from a plain program's by a relative error of at most 0.0003.
Values may be sent and summed in bfloat16 or wider, within the bound.
No kernel may reach another device: no remote copies, remote signals or barrier semaphores. Data moves between devices by JAX's collectives and lax.ppermute only.
A program may use at most 64 MiB of HBM per device.

v0:
```python
import jax
import jax.numpy as jnp
from jax import lax
from jax.sharding import PartitionSpec as P

TILE = 128
epsilon = 1e-06


def tile_layout(tile_count, last_fill, total_tiles, tile_len):
    starts = jnp.cumsum(tile_count) - tile_count
    last_tile = starts + tile_count - 1
    tile_fill = jnp.full((total_tiles,), tile_len, jnp.int32).at[last_tile].set(last_fill)
    return (starts, tile_fill)


def decode(picked, residual_codes, bucket_weights):
    residual = jnp.zeros(residual_codes.shape, jnp.float32)
    for bucket in range(4):
        residual = residual + jnp.where(
            residual_codes == bucket, bucket_weights[bucket][None, :], jnp.float32(0.0)
        )
    summed = picked.astype(jnp.float32) + residual
    scale = lax.rsqrt(jnp.sum(summed * summed, axis=1, keepdims=True) + epsilon)
    return (summed * scale).astype(jnp.bfloat16)


def assemble(own_maxima, candidates, starts, total_tiles, query_len):
    num_queries, num_cand = candidates.shape
    marker = jnp.zeros((total_tiles,), jnp.int32).at[starts].add(1)
    owner_id = jnp.cumsum(marker)
    same_next = jnp.concatenate([owner_id[1:] == owner_id[:-1], jnp.zeros((1,), bool)])
    same_after = jnp.concatenate([owner_id[2:] == owner_id[:-2], jnp.zeros((2,), bool)])
    shifted_one = jnp.concatenate([own_maxima[:, 1:], own_maxima[:, :1]], axis=1)
    shifted_two = jnp.concatenate([own_maxima[:, 2:], own_maxima[:, :2]], axis=1)
    combined = jnp.maximum(own_maxima, jnp.where(same_next[None, :], shifted_one, own_maxima))
    combined = jnp.maximum(combined, jnp.where(same_after[None, :], shifted_two, own_maxima))
    combined = combined.reshape(num_queries, query_len, total_tiles)
    first_tile = starts[candidates]
    selector = (
        first_tile[:, :, None] == jnp.arange(total_tiles, dtype=jnp.int32)[None, None, :]
    ).astype(jnp.float32)
    return jnp.einsum(
        "qit,qct->qc",
        combined,
        selector,
        precision=lax.Precision.HIGHEST,
        preferred_element_type=jnp.float32,
    )


def per_device(
    queries,
    candidates,
    centroids,
    bucket_weights,
    centroid_shard,
    centroid_row,
    residual_codes,
    tile_count,
    last_fill,
):
    n_psg = lax.axis_size("psg")
    shard_index = lax.axis_index("psg")
    tok_dev = residual_codes.shape[0]
    tiles_dev = tok_dev // TILE
    cent_dev = centroids.shape[0]
    owners = centroid_shard[:, 0]
    codebook = lax.all_gather(centroids, "psg", axis=0, tiled=True)
    picked = jnp.take(codebook, owners * cent_dev + centroid_row, axis=0)
    embedded = decode(picked, residual_codes, bucket_weights)
    total_tiles = tiles_dev * n_psg
    starts, tile_fill = tile_layout(tile_count, last_fill, total_tiles, TILE)
    local_fill = lax.dynamic_slice_in_dim(tile_fill, shard_index * tiles_dev, tiles_dev, 0)
    token_mask = jnp.arange(TILE, dtype=jnp.int32)[None, :] < local_fill[:, None]
    pad_bias = jnp.where(token_mask, jnp.float32(0.0), -jnp.inf).reshape(-1)
    per_block = max(1, 512 // TILE)
    while tiles_dev % per_block:
        per_block -= 1
    width = per_block * TILE
    piece = lax.all_gather(queries, "psg", axis=0, tiled=True)
    flat_rows = piece.reshape(-1, piece.shape[-1])
    pieces = []
    for block in range(tiles_dev // per_block):
        key_block = embedded[block * width : (block + 1) * width]
        block_scores = jnp.einsum(
            "qd,kd->qk", flat_rows, key_block, preferred_element_type=jnp.float32
        )
        block_scores = block_scores + pad_bias[block * width : (block + 1) * width][None, :]
        pieces.append(jnp.max(block_scores.reshape(flat_rows.shape[0], per_block, TILE), axis=2))
    maxima = jnp.concatenate(pieces, axis=1)
    own_maxima = lax.all_to_all(maxima, "psg", split_axis=0, concat_axis=1, tiled=True)
    return assemble(own_maxima, candidates, starts, total_tiles, queries.shape[1])


def solution(mesh):
    placed = (
        P(("groups", "psg"), None, None),
        P(("groups", "psg"), None),
        P("psg", None),
        P(),
        P("psg", None),
        P("psg"),
        P("psg", None),
        P(),
        P(),
    )
    return jax.shard_map(
        per_device,
        mesh=mesh,
        in_specs=placed,
        out_specs=P(("groups", "psg"), None),
        check_vma=False,
    )
```

profile of v0, /device:TPU:0, one launch (start us, length us, event | category | flops | bytes accessed | tf_op | source)
XLA Modules:
  0.0 90.6 jit_solution(17494278856567617430)
XLA Ops:
  6.5 0.7 all-gather.2.cloned.1.call-update
  7.3 0.7 pad_bitcast_fusion
  7.9 0.3 reduce-window.16
  8.6 0.7 compare_select_fusion.2
  9.2 1.7 %scatter_custom_fusion.1 = s32[256]{0:T(256)S(1)} fusion(s32[160]{0:T(256)S(1)} %get-tuple-element.5, s32[160]{0:T(256)S(1)} %broadcast.58, s32[]{:T(128)} %constant.21.clone.1), kind=kCustom, calls=%fused_computation.54 | custom fusion | flops 160 | bytes 1028 | tf_op jit(solution)/shard_map/scatter-add | solution.py:30
  10.9 0.3 reduce-window.24
  11.3 0.7 fusion.9
  12.0 1.2 %scatter_custom_fusion = s32[256]{0:T(256)S(1)} fusion(s32[160]{0:T(256)S(1)} %get-tuple-element.17, s32[160]{0:T(256)} %param.17, s32[]{:T(128)} %constant.15.clone.1), kind=kCustom, calls=%fused_computation.56 | custom fusion | bytes 1536 | tf_op jit(solution)/shard_map/scatter | solution.py:13
  13.5 24.3 %all_gather.7 = bf16[32,32,128]{2,1,0:T(8,128)(2,1)S(1)} all-gather(bf16[2,32,128]{2,1,0:T(8,128)(2,1)} %param.9), channel_id=1, replica_groups=mesh['groups'=2,'psg'=16] {'psg'}, dimensions={0}, use_global_device_ids=true | all-gather | bytes 278528 | tf_op jit(solution)/shard_map/all_gather | solution.py:81
  38.0 0.8 slice_bitcast_fusion.7
  38.9 0.7 broadcast_multiply_fusion
  39.6 0.7 compare_and_fusion
  40.3 0.7 broadcast_clamp_fusion
  41.0 13.0 %all-gather.2.cloned.1.call-done = bf16[8192,128]{1,0:T(8,128)(2,1)} async-done(((bf16[512,128]{1,0:T(8,128)(2,1)}), bf16[8192,128]{1,0:T(8,128)(2,1)}) %all-gather.2.cloned.1.call-update) | async-done | bytes 2097168 | tf_op jit(solution)/shard_map/all_gather | solution.py:69
  54.0 7.5 %gather_fusion = bf16[2048,128]{1,0:T(8,128)(2,1)S(1)} fusion(bf16[8192,128]{1,0:T(8,128)(2,1)} %all-gather.2.cloned.1.call-done, s32[2048]{0:T(1024)S(1)} %broadcast_clamp_fusion), kind=kCustom, calls=%fused_computation | custom fusion | bytes 1056768 | tf_op jit(solution)/shard_map/jit(_take)/gather | solution.py:70
  61.5 0.9 multiply_reduce_fusion
  62.4 0.3 multiply_convert_fusion
  62.8 0.5 bitcast_reduce_fusion.3
  63.2 0.5 bitcast_reduce_fusion.2
  63.7 0.5 bitcast_reduce_fusion.1
  64.2 0.5 bitcast_reduce_fusion
  64.8 0.7 reshape.153
  65.5 3.5 %all-to-all-start = ((f32[16,1,1024]{2,1,0:T(1,128)}), f32[16,1,1024]{2,1,0:T(1,128)S(1)}, u32[]{:S(2)}, u32[]{:S(2)}) async-start(f32[16,1,1024]{2,1,0:T(1,128)} %reshape.153), calls=%async_computation | async-start | bytes 131072 | tf_op jit(solution)/shard_map/all_to_all | solution.py:92
  69.1 6.8 %gather_fusion.1 = s32[1024]{0:T(1024)S(1)} fusion(s32[160]{0:T(256)S(1)} %get-tuple-element.6, s32[1024]{0:T(1024)S(1)} %broadcast_clamp_fusion.1), kind=kCustom, calls=%fused_computation.1 | custom fusion | bytes 12288 | tf_op jit(solution)/shard_map/gather | solution.py:39
  76.0 0.5 broadcast.78
  76.6 0.8 reduce.8
  77.6 0.2 copy.29
  77.9 0.2 copy.31
  78.0 0.2 all_to_all.19
  78.4 4.0 %fusion.3 = f32[2,256]{0,1:T(8,128)S(1)} fusion(f32[2,32,256]{1,0,2:T(2,128)S(1)} %all_to_all.19, f32[2,32,1]{1,0,2:T(2,128)S(1)} %concatenate.28, f32[2,32,255]{1,0,2:T(2,128)S(1)} %copy.29, f32[2,32,2]{1,0,2:T(2,128)S(1)} %concatenate.32, f32[2,32,254]{1,0,2:T(2,128)S(1)} %copy.31, pred[256]{0:T(512)(128)(4,1)S(1)} %concatenate.30, ...), kind=kLoop, calls=%fused_computation.20 | loop fusion | flops 114176 | bytes 199168 | tf_op jit(solution)/shard_map/qit,qct->qc/reduce_sum | solution.py:43
  82.5 0.6 fusion
  83.1 0.6 copy.37
  (38 shorter events, 1.7 us)
Async XLA Ops:
  6.5 47.5 %all-gather.2.cloned.1.call-start = ((), (), s32[]{:S(2)}) async-start(), calls=%async_computation.1 | async-start | bytes 2228224 | tf_op jit(solution)/shard_map/all_gather | solution.py:69
  41.0 20.5 %copy-start = (s32[2048,128]{1,0:T(8,128)S(1)}, s32[2048,128]{1,0:T(8,128)}, u32[]{:S(2)}) copy-start(s32[2048,128]{1,0:T(8,128)} %param.15) | copy-start | bytes 3145732
  65.5 10.5 %all-to-all-start = ((f32[16,1,1024]{2,1,0:T(1,128)}), f32[16,1,1024]{2,1,0:T(1,128)S(1)}, u32[]{:S(2)}, u32[]{:S(2)}) async-start(f32[16,1,1024]{2,1,0:T(1,128)} %reshape.153), calls=%async_computation | async-start | bytes 131072 | tf_op jit(solution)/shard_map/all_to_all | solution.py:92
Sparse Core Ops, SparseCore 0:
  9.5 44.4 all-gather.1
where the time goes:
time: 91.1 us; the launch traced here: 90.6 us
  blocking collectives  24.3 us (27%)
  local copies, waits for them, and re-layouts  20.6 us (23%)
  waiting for transfers between devices  13.8 us (15%)
  between operations  13.6 us (15%)
  other arithmetic  12.4 us (14%)
  starting transfers between devices  3.5 us (4%)
  matrix products  2.45 us (3%)
    all_gather x1, blocking collectives, per_device(): piece = lax.all_gather(queries, 'psg', axis=0, tiled=True)  24.3 us
    all_gather x1, waiting for transfers between devices, per_device(): codebook = lax.all_gather(centroids, 'psg', axis=0, tiled=True)  13 us
    gather x1, local copies, waits for them, and re-layouts, per_device(): picked = jnp.take(codebook, owners * cent_dev + centroid_row, axis=0)  7.45 us
    gather x2, local copies, waits for them, and re-layouts, assemble(): first_tile = starts[candidates]  6.83 us
    reduce_sum x1, other arithmetic, assemble(): jnp.einsum('qit,qct->qc', combined, selector, precision=lax.Precision.HIG...  4.02 us
    all_to_all x1, starting transfers between devices, per_device(): lax.all_to_all(maxima, 'psg', split_axis=0, concat_axis=1, tiled=True)  3.5 us
    dot_general x4, matrix products, per_device(): jnp.einsum('qd,kd->qk', flat_rows, key_block, preferred_element_type=jnp....  1.83 us
  transfers between devices with their start and end apart: 2, of which 1 were waited for; matrix products, arithmetic and copies ran while one was open for 18% of the time, Pallas kernels for 0%

commit v1 on v0

--- a/solution.py
+++ b/solution.py
@@ -5,6 +5,25 @@
 
 TILE = 128
 epsilon = 1e-06
+
+
+def _reach_cubes(piece_in, shard_axis):
+    current_value, high = (jax.lax.axis_size(shard_axis), jax.lax.axis_index(shard_axis))
+    parts_out = piece_in.shape[0] // current_value
+    reply = list(piece_in.shape)
+    reply[0] = parts_out
+    v1 = reply[1]
+    reply[1] = v1 * current_value
+    small = jnp.zeros(reply, piece_in.dtype)
+    for i in range(current_value):
+        outcome_arr = lax.dynamic_slice_in_dim(piece_in, (high ^ i) * parts_out, parts_out, axis=0)
+        if i:
+            xs_all = []
+            for dev_i in range(current_value):
+                xs_all.append((dev_i, dev_i ^ i))
+            outcome_arr = jax.lax.ppermute(outcome_arr, axis_name=shard_axis, perm=xs_all)
+        small = lax.dynamic_update_slice_in_dim(small, outcome_arr, (high ^ i) * v1, axis=1)
+    return small
 
 
 def tile_layout(tile_count, last_fill, total_tiles, tile_len):
@@ -89,7 +108,7 @@
         block_scores = block_scores + pad_bias[block * width : (block + 1) * width][None, :]
         pieces.append(jnp.max(block_scores.reshape(flat_rows.shape[0], per_block, TILE), axis=2))
     maxima = jnp.concatenate(pieces, axis=1)
-    own_maxima = lax.all_to_all(maxima, "psg", split_axis=0, concat_axis=1, tiled=True)
+    own_maxima = _reach_cubes(maxima, "psg")
     return assemble(own_maxima, candidates, starts, total_tiles, queries.shape[1])
 
 

time: 91.1 us -> 111 us (1.22)
  starting transfers between devices: 3.5 us -> 20.7 us
  local copies, waits for them, and re-layouts: 20.6 us -> 27.9 us
  other arithmetic: 12.4 us -> 7.66 us
    ppermute x0 -> x15, starting transfers between devices: none -> 20.7 us  [_reach_cubes(): jax.lax.ppermute(outcome_arr, axis_name=shard_axis, perm=xs_all)]
    dynamic_update_slice x0 -> x16, local copies, waits for them, and re-layouts: none -> 8.1 us  [_reach_cubes(): lax.dynamic_update_slice_in_dim(small, outcome_arr, (high ^ i) * v1, axis=1)]
    reduce_sum x1, other arithmetic: 4.02 us -> 0.11 us  [assemble(): jnp.einsum('qit,qct->qc', combined, selector, precision=lax.Precision.HIG...]
    all_to_all x1 -> x0, starting transfers between devices: 3.5 us -> none  [per_device(): lax.all_to_all(maxima, 'psg', split_axis=0, concat_axis=1, tiled=True)]
  transfers between devices with their start and end apart: 2 -> 16, of which waited for: 1 -> 1; matrix products, arithmetic and copies ran while one was open for 18% -> 23% of each run, Pallas kernels for 0% -> 0%
where the time goes in v1:
time: 111 us
  local copies, waits for them, and re-layouts  27.9 us (25%)
  blocking collectives  24.4 us (22%)
  starting transfers between devices  20.7 us (19%)
  between operations  13.9 us (13%)
  waiting for transfers between devices  13.7 us (12%)
  other arithmetic  7.66 us (7%)
  matrix products  2.45 us (2%)
    all_gather x1, blocking collectives, per_device(): piece = lax.all_gather(queries, 'psg', axis=0, tiled=True)  24.4 us
    ppermute x15, starting transfers between devices, _reach_cubes(): jax.lax.ppermute(outcome_arr, axis_name=shard_axis, perm=xs_all)  20.7 us
    all_gather x1, waiting for transfers between devices, per_device(): codebook = lax.all_gather(centroids, 'psg', axis=0, tiled=True)  12.9 us
    dynamic_update_slice x16, local copies, waits for them, and re-layouts, _reach_cubes(): lax.dynamic_update_slice_in_dim(small, outcome_arr, (high ^ i) * v1, axis=1)  8.1 us
    gather x1, local copies, waits for them, and re-layouts, per_device(): picked = jnp.take(codebook, owners * cent_dev + centroid_row, axis=0)  7.45 us
    gather x2, local copies, waits for them, and re-layouts, assemble(): first_tile = starts[candidates]  6.83 us
  transfers between devices with their start and end apart: 16, of which 1 were waited for; matrix products, arithmetic and copies ran while one was open for 23% of the time, Pallas kernels for 0%

profile of v1, /device:TPU:0, one launch (start us, length us, event | category | flops | bytes accessed | tf_op | source)
XLA Modules:
  0.0 110.7 jit_solution(1458139376438223248)
XLA Ops:
  6.5 0.7 all-gather.2.cloned.1.call-update
  7.3 0.7 pad_bitcast_fusion
  8.6 0.7 compare_select_fusion.2
  9.3 1.7 %scatter_custom_fusion.1 = s32[256]{0:T(256)S(1)} fusion(s32[160]{0:T(256)S(1)} %get-tuple-element.5, s32[160]{0:T(256)S(1)} %broadcast.50, s32[]{:T(128)} %constant.36.clone.1), kind=kCustom, calls=%fused_computation.70 | custom fusion | flops 160 | bytes 1028 | tf_op jit(solution)/shard_map/scatter-add | solution.py:49
  11.4 0.7 fusion.8
  12.1 1.2 %scatter_custom_fusion = s32[256]{0:T(256)S(1)} fusion(s32[160]{0:T(256)S(1)} %get-tuple-element.33, s32[160]{0:T(256)} %param.17, s32[]{:T(128)} %constant.44.clone.1), kind=kCustom, calls=%fused_computation.72 | custom fusion | bytes 1536 | tf_op jit(solution)/shard_map/scatter | solution.py:32
  13.6 24.4 %all_gather.7 = bf16[32,32,128]{2,1,0:T(8,128)(2,1)S(1)} all-gather(bf16[2,32,128]{2,1,0:T(8,128)(2,1)} %param.9), channel_id=1, replica_groups=mesh['groups'=2,'psg'=16] {'psg'}, dimensions={0}, use_global_device_ids=true | all-gather | bytes 278528 | tf_op jit(solution)/shard_map/all_gather | solution.py:100
  38.1 0.8 slice_bitcast_fusion.7
  39.1 0.7 broadcast_multiply_fusion
  39.8 0.7 compare_and_fusion
  40.5 0.7 broadcast_clamp_fusion
  41.2 12.9 %all-gather.2.cloned.1.call-done = bf16[8192,128]{1,0:T(8,128)(2,1)} async-done(((bf16[512,128]{1,0:T(8,128)(2,1)}), bf16[8192,128]{1,0:T(8,128)(2,1)}) %all-gather.2.cloned.1.call-update) | async-done | bytes 2097168 | tf_op jit(solution)/shard_map/all_gather | solution.py:88
  54.1 7.5 %gather_fusion = bf16[2048,128]{1,0:T(8,128)(2,1)S(1)} fusion(bf16[8192,128]{1,0:T(8,128)(2,1)} %all-gather.2.cloned.1.call-done, s32[2048]{0:T(1024)S(1)} %broadcast_clamp_fusion), kind=kCustom, calls=%fused_computation | custom fusion | bytes 1056768 | tf_op jit(solution)/shard_map/jit(_take)/gather | solution.py:89
  61.6 0.9 multiply_reduce_fusion
  66.0 1.1 collective-permute-start.2
  67.6 1.6 %collective-permute-start.4 = (f32[64,16]{1,0:T(8,128)S(1)}, f32[64,16]{1,0:T(8,128)S(1)}, u32[]{:S(2)}, u32[]{:S(2)}) collective-permute-start(f32[64,16]{1,0:T(8,128)S(1)} %copy.33), channel_id=1, source_target_pairs={{0,5},{1,4},{2,7},{3,6},{4,1},{5,0},{6,3},{7,2},{8,13},{9,12},{10,... | collective-permute-start | bytes 12296 | tf_op jit(solution)/shard_map/ppermute | solution.py:24
  70.2 2.1 %collective-permute-start.6 = (f32[64,16]{1,0:T(8,128)S(1)}, f32[64,16]{1,0:T(8,128)S(1)}, u32[]{:S(2)}, u32[]{:S(2)}) collective-permute-start(f32[64,16]{1,0:T(8,128)S(1)} %copy.35), channel_id=1, source_target_pairs={{0,7},{1,6},{2,5},{3,4},{4,3},{5,2},{6,1},{7,0},{8,15},{9,14},{10,... | collective-permute-start | bytes 12296 | tf_op jit(solution)/shard_map/ppermute | solution.py:24
  72.3 0.7 collective-permute-start.7
  73.0 2.1 %collective-permute-start.8 = (f32[64,16]{1,0:T(8,128)S(1)}, f32[64,16]{1,0:T(8,128)S(1)}, u32[]{:S(2)}, u32[]{:S(2)}) collective-permute-start(f32[64,16]{1,0:T(8,128)S(1)} %copy.37), channel_id=1, source_target_pairs={{0,9},{1,8},{2,11},{3,10},{4,13},{5,12},{6,15},{7,14},{8,1},{9,0},... | collective-permute-start | bytes 12296 | tf_op jit(solution)/shard_map/ppermute | solution.py:24
  75.0 0.9 collective-permute-start.9
  76.4 2.6 %collective-permute-start.10 = (f32[64,16]{1,0:T(8,128)S(1)}, f32[64,16]{1,0:T(8,128)S(1)}, u32[]{:S(2)}, u32[]{:S(2)}) collective-permute-start(f32[64,16]{1,0:T(8,128)S(1)} %copy.39), channel_id=1, source_target_pairs={{0,11},{1,10},{2,9},{3,8},{4,15},{5,14},{6,13},{7,12},{8,3},{9,2},... | collective-permute-start | bytes 12296 | tf_op jit(solution)/shard_map/ppermute | solution.py:24
  79.0 2.1 %collective-permute-start.11 = (f32[64,16]{1,0:T(8,128)S(1)}, f32[64,16]{1,0:T(8,128)S(1)}, u32[]{:S(2)}, u32[]{:S(2)}) collective-permute-start(f32[64,16]{1,0:T(8,128)S(1)} %copy.40), channel_id=1, source_target_pairs={{0,12},{1,13},{2,14},{3,15},{4,8},{5,9},{6,10},{7,11},{8,4},{9,5},... | collective-permute-start | bytes 12296 | tf_op jit(solution)/shard_map/ppermute | solution.py:24
  81.1 1.6 %collective-permute-start.12 = (f32[64,16]{1,0:T(8,128)S(1)}, f32[64,16]{1,0:T(8,128)S(1)}, u32[]{:S(2)}, u32[]{:S(2)}) collective-permute-start(f32[64,16]{1,0:T(8,128)S(1)} %copy.41), channel_id=1, source_target_pairs={{0,13},{1,12},{2,15},{3,14},{4,9},{5,8},{6,11},{7,10},{8,5},{9,4},... | collective-permute-start | bytes 12296 | tf_op jit(solution)/shard_map/ppermute | solution.py:24
  82.7 2.0 %collective-permute-start.13 = (f32[64,16]{1,0:T(8,128)S(1)}, f32[64,16]{1,0:T(8,128)S(1)}, u32[]{:S(2)}, u32[]{:S(2)}) collective-permute-start(f32[64,16]{1,0:T(8,128)S(1)} %copy.42), channel_id=1, source_target_pairs={{0,14},{1,15},{2,12},{3,13},{4,10},{5,11},{6,8},{7,9},{8,6},{9,7},... | collective-permute-start | bytes 12296 | tf_op jit(solution)/shard_map/ppermute | solution.py:24
  84.7 2.3 %collective-permute-start.14 = (f32[64,16]{1,0:T(8,128)S(1)}, f32[64,16]{1,0:T(8,128)S(1)}, u32[]{:S(2)}, u32[]{:S(2)}) collective-permute-start(f32[64,16]{1,0:T(8,128)S(1)} %copy.43), channel_id=1, source_target_pairs={{0,15},{1,14},{2,13},{3,12},{4,11},{5,10},{6,9},{7,8},{8,7},{9,6},... | collective-permute-start | bytes 12296 | tf_op jit(solution)/shard_map/ppermute | solution.py:24
  87.0 6.8 %gather_fusion.1 = s32[1024]{0:T(1024)S(1)} fusion(s32[160]{0:T(256)S(1)} %get-tuple-element.6, s32[1024]{0:T(1024)S(1)} %broadcast_clamp_fusion.1), kind=kCustom, calls=%fused_computation.1 | custom fusion | bytes 12288 | tf_op jit(solution)/shard_map/gather | solution.py:58
  95.1 0.6 dynamic_update_slice.50
  95.7 0.6 dynamic_update_slice.51
  96.3 0.6 dynamic_update_slice.52
  96.9 0.6 dynamic_update_slice.53
  102.6 0.6 fusion
  103.2 0.6 copy.48
  (85 shorter events, 13.1 us)
Async XLA Ops:
  6.5 47.6 %all-gather.2.cloned.1.call-start = ((), (), s32[]{:S(2)}) async-start(), calls=%async_computation | async-start | bytes 2228224 | tf_op jit(solution)/shard_map/all_gather | solution.py:88
  41.2 20.4 %copy-start = (s32[2048,128]{1,0:T(8,128)S(1)}, s32[2048,128]{1,0:T(8,128)}, u32[]{:S(2)}) copy-start(s32[2048,128]{1,0:T(8,128)} %param.15) | copy-start | bytes 3145732
  65.0 4.7 %collective-permute-start = (f32[64,16]{1,0:T(8,128)S(1)}, f32[64,16]{1,0:T(8,128)S(1)}, u32[]{:S(2)}, u32[]{:S(2)}) collective-permute-start(f32[64,16]{1,0:T(8,128)S(1)} %copy.29), channel_id=1, source_target_pairs={{0,1},{1,0},{2,3},{3,2},{4,5},{5,4},{6,7},{7,6},{8,9},{9,8},{10,11... | collective-permute-start | bytes 12296 | tf_op jit(solution)/shard_map/ppermute | solution.py:24
  65.3 4.8 %collective-permute-start.1 = (f32[64,16]{1,0:T(8,128)S(1)}, f32[64,16]{1,0:T(8,128)S(1)}, u32[]{:S(2)}, u32[]{:S(2)}) collective-permute-start(f32[64,16]{1,0:T(8,128)S(1)} %copy.30), channel_id=1, source_target_pairs={{0,2},{1,3},{2,0},{3,1},{4,6},{5,7},{6,4},{7,5},{8,10},{9,11},{10,... | collective-permute-start | bytes 12296 | tf_op jit(solution)/shard_map/ppermute | solution.py:24
  66.0 6.3 %collective-permute-start.2 = (f32[64,16]{1,0:T(8,128)S(1)}, f32[64,16]{1,0:T(8,128)S(1)}, u32[]{:S(2)}, u32[]{:S(2)}) collective-permute-start(f32[64,16]{1,0:T(8,128)S(1)} %copy.31), channel_id=1, source_target_pairs={{0,3},{1,2},{2,1},{3,0},{4,7},{5,6},{6,5},{7,4},{8,11},{9,10},{10,... | collective-permute-start | bytes 12296 | tf_op jit(solution)/shard_map/ppermute | solution.py:24
  67.2 5.8 %collective-permute-start.3 = (f32[64,16]{1,0:T(8,128)S(1)}, f32[64,16]{1,0:T(8,128)S(1)}, u32[]{:S(2)}, u32[]{:S(2)}) collective-permute-start(f32[64,16]{1,0:T(8,128)S(1)} %copy.32), channel_id=1, source_target_pairs={{0,4},{1,5},{2,6},{3,7},{4,0},{5,1},{6,2},{7,3},{8,12},{9,13},{10,... | collective-permute-start | bytes 12296 | tf_op jit(solution)/shard_map/ppermute | solution.py:24
  67.6 7.4 %collective-permute-start.4 = (f32[64,16]{1,0:T(8,128)S(1)}, f32[64,16]{1,0:T(8,128)S(1)}, u32[]{:S(2)}, u32[]{:S(2)}) collective-permute-start(f32[64,16]{1,0:T(8,128)S(1)} %copy.33), channel_id=1, source_target_pairs={{0,5},{1,4},{2,7},{3,6},{4,1},{5,0},{6,3},{7,2},{8,13},{9,12},{10,... | collective-permute-start | bytes 12296 | tf_op jit(solution)/shard_map/ppermute | solution.py:24
  69.7 6.7 %collective-permute-start.5 = (f32[64,16]{1,0:T(8,128)S(1)}, f32[64,16]{1,0:T(8,128)S(1)}, u32[]{:S(2)}, u32[]{:S(2)}) collective-permute-start(f32[64,16]{1,0:T(8,128)S(1)} %copy.34), channel_id=1, source_target_pairs={{0,6},{1,7},{2,4},{3,5},{4,2},{5,3},{6,0},{7,1},{8,14},{9,15},{10,... | collective-permute-start | bytes 12296 | tf_op jit(solution)/shard_map/ppermute | solution.py:24
  70.2 8.9 %collective-permute-start.6 = (f32[64,16]{1,0:T(8,128)S(1)}, f32[64,16]{1,0:T(8,128)S(1)}, u32[]{:S(2)}, u32[]{:S(2)}) collective-permute-start(f32[64,16]{1,0:T(8,128)S(1)} %copy.35), channel_id=1, source_target_pairs={{0,7},{1,6},{2,5},{3,4},{4,3},{5,2},{6,1},{7,0},{8,15},{9,14},{10,... | collective-permute-start | bytes 12296 | tf_op jit(solution)/shard_map/ppermute | solution.py:24
  72.3 8.8 %collective-permute-start.7 = (f32[64,16]{1,0:T(8,128)S(1)}, f32[64,16]{1,0:T(8,128)S(1)}, u32[]{:S(2)}, u32[]{:S(2)}) collective-permute-start(f32[64,16]{1,0:T(8,128)S(1)} %copy.36), channel_id=1, source_target_pairs={{0,8},{1,9},{2,10},{3,11},{4,12},{5,13},{6,14},{7,15},{8,0},{9,1},... | collective-permute-start | bytes 12296 | tf_op jit(solution)/shard_map/ppermute | solution.py:24
  73.0 9.7 %collective-permute-start.8 = (f32[64,16]{1,0:T(8,128)S(1)}, f32[64,16]{1,0:T(8,128)S(1)}, u32[]{:S(2)}, u32[]{:S(2)}) collective-permute-start(f32[64,16]{1,0:T(8,128)S(1)} %copy.37), channel_id=1, source_target_pairs={{0,9},{1,8},{2,11},{3,10},{4,13},{5,12},{6,15},{7,14},{8,1},{9,0},... | collective-permute-start | bytes 12296 | tf_op jit(solution)/shard_map/ppermute | solution.py:24
  75.0 9.7 %collective-permute-start.9 = (f32[64,16]{1,0:T(8,128)S(1)}, f32[64,16]{1,0:T(8,128)S(1)}, u32[]{:S(2)}, u32[]{:S(2)}) collective-permute-start(f32[64,16]{1,0:T(8,128)S(1)} %copy.38), channel_id=1, source_target_pairs={{0,10},{1,11},{2,8},{3,9},{4,14},{5,15},{6,12},{7,13},{8,2},{9,3},... | collective-permute-start | bytes 12296 | tf_op jit(solution)/shard_map/ppermute | solution.py:24
  76.4 23.6 %collective-permute-start.10 = (f32[64,16]{1,0:T(8,128)S(1)}, f32[64,16]{1,0:T(8,128)S(1)}, u32[]{:S(2)}, u32[]{:S(2)}) collective-permute-start(f32[64,16]{1,0:T(8,128)S(1)} %copy.39), channel_id=1, source_target_pairs={{0,11},{1,10},{2,9},{3,8},{4,15},{5,14},{6,13},{7,12},{8,3},{9,2},... | collective-permute-start | bytes 12296 | tf_op jit(solution)/shard_map/ppermute | solution.py:24
  79.0 21.4 %collective-permute-start.11 = (f32[64,16]{1,0:T(8,128)S(1)}, f32[64,16]{1,0:T(8,128)S(1)}, u32[]{:S(2)}, u32[]{:S(2)}) collective-permute-start(f32[64,16]{1,0:T(8,128)S(1)} %copy.40), channel_id=1, source_target_pairs={{0,12},{1,13},{2,14},{3,15},{4,8},{5,9},{6,10},{7,11},{8,4},{9,5},... | collective-permute-start | bytes 12296 | tf_op jit(solution)/shard_map/ppermute | solution.py:24
  81.1 19.8 %collective-permute-start.12 = (f32[64,16]{1,0:T(8,128)S(1)}, f32[64,16]{1,0:T(8,128)S(1)}, u32[]{:S(2)}, u32[]{:S(2)}) collective-permute-start(f32[64,16]{1,0:T(8,128)S(1)} %copy.41), channel_id=1, source_target_pairs={{0,13},{1,12},{2,15},{3,14},{4,9},{5,8},{6,11},{7,10},{8,5},{9,4},... | collective-permute-start | bytes 12296 | tf_op jit(solution)/shard_map/ppermute | solution.py:24
  82.7 18.7 %collective-permute-start.13 = (f32[64,16]{1,0:T(8,128)S(1)}, f32[64,16]{1,0:T(8,128)S(1)}, u32[]{:S(2)}, u32[]{:S(2)}) collective-permute-start(f32[64,16]{1,0:T(8,128)S(1)} %copy.42), channel_id=1, source_target_pairs={{0,14},{1,15},{2,12},{3,13},{4,10},{5,11},{6,8},{7,9},{8,6},{9,7},... | collective-permute-start | bytes 12296 | tf_op jit(solution)/shard_map/ppermute | solution.py:24
  84.7 17.1 %collective-permute-start.14 = (f32[64,16]{1,0:T(8,128)S(1)}, f32[64,16]{1,0:T(8,128)S(1)}, u32[]{:S(2)}, u32[]{:S(2)}) collective-permute-start(f32[64,16]{1,0:T(8,128)S(1)} %copy.43), channel_id=1, source_target_pairs={{0,15},{1,14},{2,13},{3,12},{4,11},{5,10},{6,9},{7,8},{8,7},{9,6},... | collective-permute-start | bytes 12296 | tf_op jit(solution)/shard_map/ppermute | solution.py:24
Sparse Core Ops, SparseCore 0:
  9.5 44.5 all-gather.1
